TPU v7x, 32 devices: a whole 2x2x4 slice. The times are simulated.
32 devices in a mesh: parts: 2 (over y), expert: 4 (over z), tensor: 2 (over x), seq: 2 (over core).
Axes of the slice: x: 2, y: 2, z: 4, core: 2. Of those that a mesh axis runs over, the one named last changes fastest.
Arguments:
- tokens: bfloat16 [128, 4096], P(('parts', 'expert', 'tensor', 'seq')), parts along dimension 0, may hold values from -6 to 6
- out_grad: bfloat16 [128, 4096], P(('parts', 'expert', 'tensor', 'seq')), parts along dimension 0, may hold values from -3 to 3
- expert_ids: int32 [128, 2], P(('parts', 'expert', 'tensor', 'seq')), parts along dimension 0, may hold values from 0 to 3, all different within a row; in each aligned block of 4 rows (0 to 3, 4 to 7, ...) at most 3 rows name the same one
- probs: bfloat16 [128, 2], P(('parts', 'expert', 'tensor', 'seq')), parts along dimension 0, may hold values from 0.19921875 to 1
- w_gate: bfloat16 [4, 4096, 8192], P('expert', None, ('tensor', 'seq')), may hold values from -0.09375 to 0.09375
- w_up: bfloat16 [4, 4096, 8192], P('expert', None, ('tensor', 'seq')), may hold values from -0.09375 to 0.09375
- w_down: bfloat16 [4, 8192, 4096], P('expert', ('tensor', 'seq')), may hold values from -0.0625 to 0.0625
Outputs:
- grad_tokens: float32 [128, 4096], P(('parts', 'expert', 'tensor', 'seq')), parts along dimension 0
- grad_probs: float32 [128, 2], P(('parts', 'expert', 'tensor', 'seq')), parts along dimension 0
- grad_gate: bfloat16 [8, 4096, 8192], P(('parts', 'expert'), None, ('tensor', 'seq')), parts along dimension 0
- grad_up: bfloat16 [8, 4096, 8192], P(('parts', 'expert'), None, ('tensor', 'seq')), parts along dimension 0
- grad_down: bfloat16 [8, 8192, 4096], P(('parts', 'expert'), ('tensor', 'seq')), parts along dimension 0
There are 2 independent parts, one for each index of `parts`. A program takes and returns all parts, laid end to end along the dimension named above; an argument that names none is the same for every part. Nothing has to cross between parts.
Inputs may be any that keep to these rules, and one draw needn't show every extreme that they name: `expert_ids`: each row names 2 different experts. Within the rows of one device (aligned blocks of 4 rows) no expert is named by more than 3 rows, a bound that some block reaches.
All inputs are finite; a program needn't handle non-finite values.
Results may differ from a plain program's by a relative error of at most 0.005.
Values may be sent and summed in bfloat16 or wider, within the bound.
No kernel may reach another device: no remote copies, remote signals or barrier semaphores. Data moves between devices by JAX's collectives and lax.ppermute only.
A program may use at most 192 MiB of HBM per device.

v0:
```python
import jax
import jax.numpy as jnp
from jax import lax
from jax.sharding import PartitionSpec as P

EXPERTS = 4
TOP = 2
CAP = 3


def silu_parts(gate):
    sigma = jax.nn.sigmoid(gate)
    return (gate * sigma, sigma * (1.0 + gate * (1.0 - sigma)))


def repeat_owners(block, copies):
    shape = block.shape
    wide = jnp.broadcast_to(block[:, None], (shape[0], copies) + shape[1:])
    return wide.reshape((shape[0] * copies,) + shape[1:])


def contract(left, right, left_dim, right_dim):
    return lax.dot_general(
        left, right, (((left_dim,), (right_dim,)), ((), ())), preferred_element_type=jnp.float32
    )


def per_device(tokens, out_grad, expert_ids, probs, w_gate, w_up, w_down):
    owners = lax.axis_size("expert")
    holders = lax.axis_size(("tensor", "seq"))
    split = owners // EXPERTS
    width = tokens.shape[1]
    count = tokens.shape[0]
    flat = expert_ids.reshape(-1)
    onehot = (flat[:, None] == jnp.arange(EXPERTS, dtype=jnp.int32)[None, :]).astype(jnp.int32)
    before = jnp.cumsum(onehot, axis=0) - onehot
    target = flat * CAP + jnp.sum(before * onehot, axis=1)
    places = jnp.arange(EXPERTS * CAP, dtype=jnp.int32)
    hits = places[:, None] == target[None, :]
    select = jnp.any(hits.reshape(EXPERTS * CAP, count, TOP), axis=2).astype(jnp.bfloat16)
    packed_x = (
        jnp.dot(select, tokens, preferred_element_type=jnp.float32)
        .astype(jnp.bfloat16)
        .reshape(EXPERTS, CAP, width)
    )
    packed_dy = (
        jnp.dot(select, out_grad, preferred_element_type=jnp.float32)
        .astype(jnp.bfloat16)
        .reshape(EXPERTS, CAP, width)
    )
    weights_flat = probs.reshape(-1).astype(jnp.float32)
    packed_p = (
        jnp.sum(jnp.where(hits, weights_flat[None, :], 0.0), axis=1)
        .astype(jnp.bfloat16)
        .reshape(EXPERTS, CAP)
    )
    fanout = split * holders
    rows_x, rows_dy, rows_p = (
        lax.all_to_all(
            repeat_owners(packed_x, fanout),
            ("expert", "tensor", "seq"),
            split_axis=0,
            concat_axis=0,
            tiled=True,
        ),
        lax.all_to_all(
            repeat_owners(packed_dy, fanout),
            ("expert", "tensor", "seq"),
            split_axis=0,
            concat_axis=0,
            tiled=True,
        ),
        lax.all_to_all(
            repeat_owners(packed_p, fanout),
            ("expert", "tensor", "seq"),
            split_axis=0,
            concat_axis=0,
            tiled=True,
        ),
    )
    inputs = rows_x.reshape(-1, width)
    cotangent = rows_dy.reshape(-1, width)
    scale = rows_p.reshape(-1, 1).astype(jnp.float32)
    w_g = w_gate[0]
    w_u = w_up[0]
    w_d = w_down[0]
    gate = jnp.dot(inputs, w_g, preferred_element_type=jnp.float32)
    up = jnp.dot(inputs, w_u, preferred_element_type=jnp.float32)
    back = contract(cotangent, w_d, 1, 1)
    act, slope = silu_parts(gate)
    hidden = act * up
    score = jnp.sum(back * hidden, axis=1)
    scaled = scale * back
    d_gate = (scaled * up * slope).astype(jnp.bfloat16)
    d_up = (scaled * act).astype(jnp.bfloat16)
    weighted = (scale * hidden).astype(jnp.bfloat16)
    part_dx = contract(d_gate, w_g, 1, 1) + contract(d_up, w_u, 1, 1)
    grad_g = contract(inputs, d_gate, 0, 0).astype(jnp.bfloat16)[None]
    grad_u = contract(inputs, d_up, 0, 0).astype(jnp.bfloat16)[None]
    grad_d = contract(weighted, cotangent, 0, 0).astype(jnp.bfloat16)[None]
    blocks = owners * holders
    got_dx, got_score = (
        lax.all_to_all(
            part_dx.reshape(blocks, CAP, width),
            ("expert", "tensor", "seq"),
            split_axis=0,
            concat_axis=0,
            tiled=True,
        ),
        lax.all_to_all(
            score.reshape(blocks, CAP),
            ("expert", "tensor", "seq"),
            split_axis=0,
            concat_axis=0,
            tiled=True,
        ),
    )
    total_dx = jnp.sum(got_dx.reshape(EXPERTS, split * holders, CAP, width), axis=1).reshape(
        EXPERTS * CAP, width
    )
    total_score = jnp.sum(got_score.reshape(EXPERTS, split * holders, CAP), axis=1).reshape(-1)
    grad_tokens = jnp.sum(jnp.take(total_dx, target, axis=0).reshape(count, TOP, width), axis=1)
    grad_probs = jnp.take(total_score, target, axis=0).reshape(count, TOP)
    return (grad_tokens, grad_probs, grad_g, grad_u, grad_d)


def solution(mesh):
    placed = (
        P(("parts", "expert", "tensor", "seq"), None),
        P(("parts", "expert", "tensor", "seq"), None),
        P(("parts", "expert", "tensor", "seq"), None),
        P(("parts", "expert", "tensor", "seq"), None),
        P("expert", None, ("tensor", "seq")),
        P("expert", None, ("tensor", "seq")),
        P("expert", ("tensor", "seq"), None),
    )
    return jax.shard_map(
        per_device,
        mesh=mesh,
        in_specs=placed,
        out_specs=(
            P(("parts", "expert", "tensor", "seq"), None),
            P(("parts", "expert", "tensor", "seq"), None),
            P(("parts", "expert"), None, ("tensor", "seq")),
            P(("parts", "expert"), None, ("tensor", "seq")),
            P(("parts", "expert"), ("tensor", "seq"), None),
        ),
        check_vma=False,
    )
```

profile of v0, /device:TPU:0, one launch (start us, length us, event | category | flops | bytes accessed | tf_op | source)
XLA Modules:
  0.0 131.7 jit_solution(5877994073357987897)
XLA Ops:
  0.6 0.8 copy.35
  1.4 0.1 reshape.140
  1.5 0.2 reduce_window_sum.11
  1.7 0.7 copy.37
  2.5 0.1 reshape.150
  2.6 0.1 select_reduce_fusion.1
  2.7 0.1 convert_element_type.63
  2.7 0.1 copy.38
  2.9 0.1 all_to_all.21
  3.0 0.7 copy.39
  3.7 7.4 %all-to-all-start = ((bf16[16,1,3]{2,1,0:T(2,128)(2,1)}), bf16[16,1,3]{2,1,0:T(2,128)(2,1)S(1)}, u32[]{:S(2)}, u32[]{:S(2)}) async-start(bf16[16,1,3]{2,1,0:T(2,128)(2,1)} %copy.39), calls=%async_computation | async-start | bytes 16384 | tf_op jit(solution)/shard_map/all_to_all | solution.py:73
  11.2 0.1 copy.40
  11.3 0.1 fusion.16
  11.4 0.2 convolution_convert_fusion
  11.7 5.8 %all-to-all-done = bf16[16,1,3]{2,1,0:T(2,128)(2,1)S(1)} async-done(((bf16[16,1,3]{2,1,0:T(2,128)(2,1)}), bf16[16,1,3]{2,1,0:T(2,128)(2,1)S(1)}, u32[]{:S(2)}, u32[]{:S(2)}) %all-to-all-start) | async-done | bytes 128 | tf_op jit(solution)/shard_map/all_to_all | solution.py:73
  17.5 1.0 broadcast_in_dim.63
  18.5 3.6 %all-to-all-start.2 = ((bf16[16,3,4096]{2,1,0:T(4,128)(2,1)}), bf16[16,3,4096]{2,1,0:T(4,128)(2,1)S(1)}, u32[]{:S(2)}, u32[]{:S(2)}) async-start(bf16[16,3,4096]{2,1,0:T(4,128)(2,1)} %bitcast.2), calls=%async_computation.2 | async-start | bytes 1048576 | tf_op jit(solution)/shard_map/all_to_all | solution.py:59
  22.1 0.1 mul.76
  22.1 1.0 convolution_convert_fusion.1
  23.3 0.1 reshape.151
  23.3 12.9 %all-to-all-done.2 = bf16[16,3,4096]{2,1,0:T(4,128)(2,1)S(1)} async-done(((bf16[16,3,4096]{2,1,0:T(4,128)(2,1)}), bf16[16,3,4096]{2,1,0:T(4,128)(2,1)S(1)}, u32[]{:S(2)}, u32[]{:S(2)}) %all-to-all-start.2) | async-done | bytes 393248 | tf_op jit(solution)/shard_map/all_to_all | solution.py:59
  36.3 1.0 broadcast_in_dim.61
  37.3 4.1 %all-to-all-start.1 = ((bf16[16,3,4096]{2,1,0:T(4,128)(2,1)}), bf16[16,3,4096]{2,1,0:T(4,128)(2,1)S(1)}, u32[]{:S(2)}, u32[]{:S(2)}) async-start(bf16[16,3,4096]{2,1,0:T(4,128)(2,1)} %bitcast), calls=%async_computation.1 | async-start | bytes 1048576 | tf_op jit(solution)/shard_map/all_to_all | solution.py:66
  41.4 0.3 reshape.144
  41.7 8.9 %fusion.2 = f32[48,2048]{1,0:T(8,128)S(1)} fusion(bf16[48,4096]{1,0:T(8,128)(2,1)S(1)} %reshape.144, bf16[1,4096,2048]{2,1,0:T(8,128)(2,1)} %param.11), kind=kOutput, calls=%fused_computation.4 | convolution fusion | flops 805306368 | bytes 17563648 | tf_op jit(solution)/shard_map/dot_general | solution.py:87
  50.7 1.6 %copy-done.2 = bf16[1,4096,2048]{2,1,0:T(8,128)(2,1)S(1)} copy-done((bf16[1,4096,2048]{2,1,0:T(8,128)(2,1)S(1)}, bf16[1,4096,2048]{2,1,0:T(8,128)(2,1)}, u32[]{:S(2)}) %copy-start.2) | copy-done | bytes 16777240
  52.3 3.1 %fusion.6 = f32[48,2048]{1,0:T(8,128)S(1)} fusion(bf16[48,4096]{1,0:T(8,128)(2,1)S(1)} %reshape.144, bf16[1,4096,2048]{2,1,0:T(8,128)(2,1)S(1)} %copy-done.2), kind=kOutput, calls=%fused_computation.8 | convolution fusion | flops 805306368 | bytes 17563648 | tf_op jit(solution)/shard_map/dot_general | solution.py:88
  55.3 0.3 all-to-all-done.1
  55.7 0.3 reshape.142
  56.0 11.0 %multiply_reduce_fusion = (f32[48]{0:T(128)S(1)}, bf16[48,2048]{1,0:T(8,128)(2,1)S(1)}, bf16[48,2048]{1,0:T(8,128)(2,1)S(1)}) fusion(f32[48,2048]{1,0:T(8,128)S(1)} %fusion.6, f32[48,2048]{1,0:T(8,128)S(1)} %fusion.2, f32[48]{0:T(128)S(1)} %reshape.151, bf16[48,4096]{1,0:T(8,128)(2,1)S(1)} %reshape.142, bf16[1,2048,4096]{2,1,0:T(8,128)(2,1)} %param.13), kind=kOutput, calls=%fused_computation.20 | convolution fusion | flops 806977472 | bytes 18350464 | tf_op jit(solution)/shard_map/dot_general | solution.py:23
  67.1 0.7 all_to_all.26
  67.7 5.7 %all-to-all-start.4 = ((f32[16,1,3]{2,1,0:T(1,128)}), f32[16,1,3]{2,1,0:T(1,128)S(1)}, u32[]{:S(2)}, u32[]{:S(2)}) async-start(f32[16,1,3]{2,1,0:T(1,128)} %bitcast.8), calls=%async_computation.4 | async-start | bytes 16384 | tf_op jit(solution)/shard_map/all_to_all | solution.py:110
  73.5 10.9 %fusion = f32[48,4096]{1,0:T(8,128)S(1)} fusion(bf16[48,2048]{1,0:T(8,128)(2,1)S(1)} %get-tuple-element.28, bf16[1,4096,2048]{2,1,0:T(8,128)(2,1)} %param.11), kind=kOutput, calls=%fused_computation.2 | convolution fusion | flops 805306368 | bytes 17760256 | tf_op jit(solution)/shard_map/dot_general | solution.py:23
  84.4 10.9 %fusion.10 = f32[48,4096]{1,0:T(8,128)S(1)} fusion(f32[48,4096]{1,0:T(8,128)S(1)} %fusion, bf16[48,2048]{1,0:T(8,128)(2,1)S(1)} %get-tuple-element.29, bf16[1,4096,2048]{2,1,0:T(8,128)(2,1)} %param.12), kind=kOutput, calls=%fused_computation.15 | convolution fusion | flops 805502976 | bytes 18546688 | tf_op jit(solution)/shard_map/dot_general | solution.py:23
  95.3 1.3 %reshape.145 = f32[16,3,4096]{2,1,0:T(4,128)} reshape(f32[48,4096]{1,0:T(8,128)S(1)} %fusion.10) | data formatting | bytes 1572864 | tf_op jit(solution)/shard_map/reshape | solution.py:104
  96.6 6.0 %all-to-all-start.3 = ((f32[16,3,4096]{2,1,0:T(4,128)}), f32[16,3,4096]{2,1,0:T(4,128)S(1)}, u32[]{:S(2)}, u32[]{:S(2)}) async-start(f32[16,3,4096]{2,1,0:T(4,128)} %reshape.145), calls=%async_computation.3 | async-start | bytes 2097152 | tf_op jit(solution)/shard_map/all_to_all | solution.py:103
  102.7 8.6 %convert_bitcast_fusion = bf16[1,2048,4096]{2,1,0:T(8,128)(2,1)} fusion(bf16[48,4096]{1,0:T(8,128)(2,1)S(1)} %reshape.142, f32[48]{0:T(128)S(1)} %reshape.151, f32[48,2048]{1,0:T(8,128)S(1)} %fusion.6, f32[48,2048]{1,0:T(8,128)S(1)} %fusion.2), kind=kOutput, calls=%fused_computation.12 | convolution fusion | flops 814383104 | bytes 17957056 | tf_op jit(solution)/shard_map/dot_general | solution.py:23
  111.3 8.5 %convert_bitcast_fusion.1 = bf16[1,4096,2048]{2,1,0:T(8,128)(2,1)} fusion(bf16[48,4096]{1,0:T(8,128)(2,1)S(1)} %reshape.144, bf16[48,2048]{1,0:T(8,128)(2,1)S(1)} %get-tuple-element.29), kind=kOutput, calls=%fused_computation.13 | convolution fusion | flops 813694976 | bytes 17367040 | tf_op jit(solution)/shard_map/dot_general | solution.py:23
  119.8 8.5 %convert_bitcast_fusion.2 = bf16[1,4096,2048]{2,1,0:T(8,128)(2,1)} fusion(bf16[48,4096]{1,0:T(8,128)(2,1)S(1)} %reshape.144, bf16[48,2048]{1,0:T(8,128)(2,1)S(1)} %copy-done.4), kind=kOutput, calls=%fused_computation.14 | convolution fusion | flops 813694976 | bytes 17367040 | tf_op jit(solution)/shard_map/dot_general | solution.py:23
  128.4 0.1 reshape.149
  128.5 0.6 gather_fusion.1
  129.1 0.1 gather.15
  129.2 0.7 copy.44
  129.9 0.2 bitcast_reduce_fusion
  130.0 0.1 reshape.147
  130.1 0.6 gather_fusion
  130.7 0.1 gather.13
  130.8 0.9 select_reduce_fusion
  (24 shorter events, 0.5 us)
Async XLA Ops:
  0.6 10.8 %copy-start = (bf16[4,4096]{1,0:T(4,128)(2,1)S(1)}, bf16[4,4096]{1,0:T(4,128)(2,1)}, u32[]{:S(2)}) copy-start(bf16[4,4096]{1,0:T(4,128)(2,1)} %param.7) | copy-start | bytes 98308
  3.7 13.8 %all-to-all-start = ((bf16[16,1,3]{2,1,0:T(2,128)(2,1)}), bf16[16,1,3]{2,1,0:T(2,128)(2,1)S(1)}, u32[]{:S(2)}, u32[]{:S(2)}) async-start(bf16[16,1,3]{2,1,0:T(2,128)(2,1)} %copy.39), calls=%async_computation | async-start | bytes 16384 | tf_op jit(solution)/shard_map/all_to_all | solution.py:73
  18.5 17.8 %all-to-all-start.2 = ((bf16[16,3,4096]{2,1,0:T(4,128)(2,1)}), bf16[16,3,4096]{2,1,0:T(4,128)(2,1)S(1)}, u32[]{:S(2)}, u32[]{:S(2)}) async-start(bf16[16,3,4096]{2,1,0:T(4,128)(2,1)} %bitcast.2), calls=%async_computation.2 | async-start | bytes 1048576 | tf_op jit(solution)/shard_map/all_to_all | solution.py:59
  37.3 18.4 %all-to-all-start.1 = ((bf16[16,3,4096]{2,1,0:T(4,128)(2,1)}), bf16[16,3,4096]{2,1,0:T(4,128)(2,1)S(1)}, u32[]{:S(2)}, u32[]{:S(2)}) async-start(bf16[16,3,4096]{2,1,0:T(4,128)(2,1)} %bitcast), calls=%async_computation.1 | async-start | bytes 1048576 | tf_op jit(solution)/shard_map/all_to_all | solution.py:66
  41.7 10.5 %copy-start.2 = (bf16[1,4096,2048]{2,1,0:T(8,128)(2,1)S(1)}, bf16[1,4096,2048]{2,1,0:T(8,128)(2,1)}, u32[]{:S(2)}) copy-start(bf16[1,4096,2048]{2,1,0:T(8,128)(2,1)} %param.12) | copy-start | bytes 50331652
  67.0 28.3 %copy-start.3 = (bf16[48,2048]{1,0:T(8,128)(2,1)}, bf16[48,2048]{1,0:T(8,128)(2,1)S(1)}, u32[]{:S(2)}) copy-start(bf16[48,2048]{1,0:T(8,128)(2,1)S(1)} %get-tuple-element.28) | copy-start | bytes 589828
  67.7 28.9 %all-to-all-start.4 = ((f32[16,1,3]{2,1,0:T(1,128)}), f32[16,1,3]{2,1,0:T(1,128)S(1)}, u32[]{:S(2)}, u32[]{:S(2)}) async-start(f32[16,1,3]{2,1,0:T(1,128)} %bitcast.8), calls=%async_computation.4 | async-start | bytes 16384 | tf_op jit(solution)/shard_map/all_to_all | solution.py:110
  96.6 33.2 %all-to-all-start.3 = ((f32[16,3,4096]{2,1,0:T(4,128)}), f32[16,3,4096]{2,1,0:T(4,128)S(1)}, u32[]{:S(2)}, u32[]{:S(2)}) async-start(f32[16,3,4096]{2,1,0:T(4,128)} %reshape.145), calls=%async_computation.3 | async-start | bytes 2097152 | tf_op jit(solution)/shard_map/all_to_all | solution.py:103
  102.7 17.2 %copy-start.4 = (bf16[48,2048]{1,0:T(8,128)(2,1)S(1)}, bf16[48,2048]{1,0:T(8,128)(2,1)}, u32[]{:S(2)}) copy-start(bf16[48,2048]{1,0:T(8,128)(2,1)} %copy-done.3) | copy-start | bytes 589828
  102.7 29.0 %copy-start.1 = (bf16[4,4096]{1,0:T(4,128)(2,1)S(1)}, bf16[4,4096]{1,0:T(4,128)(2,1)}, u32[]{:S(2)}) copy-start(bf16[4,4096]{1,0:T(4,128)(2,1)} %param.7) | copy-start | bytes 98308
where the time goes:
time: 132 us
  matrix products  71.8 us (54%)
  starting transfers between devices  26.8 us (20%)
  waiting for transfers between devices  19 us (14%)
  local copies, waits for them, and re-layouts  11.8 us (9%)
  other arithmetic  1.51 us (1%)
    dot_general x6, matrix products, contract(): lax.dot_general(left, right, (((left_dim,), (right_dim,)), ((), ())), pre...  58.5 us
    all_to_all x1, waiting for transfers between devices, per_device(): lax.all_to_all(repeat_owners(packed_x, fanout), ('expert', 'tensor', 'seq...  12.9 us
    dot_general x1, matrix products, per_device(): gate = jnp.dot(inputs, w_g, preferred_element_type=jnp.float32)  8.94 us
    all_to_all x1, starting transfers between devices, per_device(): lax.all_to_all(repeat_owners(packed_p, fanout), ('expert', 'tensor', 'seq...  7.39 us
    all_to_all x1, starting transfers between devices, per_device(): lax.all_to_all(part_dx.reshape(blocks, CAP, width), ('expert', 'tensor',...  6.01 us
    all_to_all x1, waiting for transfers between devices, per_device(): lax.all_to_all(repeat_owners(packed_p, fanout), ('expert', 'tensor', 'seq...  5.76 us
    all_to_all x1, starting transfers between devices, per_device(): lax.all_to_all(score.reshape(blocks, CAP), ('expert', 'tensor', 'seq'), s...  5.7 us
    all_to_all x1, starting transfers between devices, per_device(): lax.all_to_all(repeat_owners(packed_dy, fanout), ('expert', 'tensor', 'se...  4.09 us
  transfers between devices with their start and end apart: 5, of which 3 were waited for; matrix products, arithmetic and copies ran while one was open for 49% of the time, Pallas kernels for 0%

commit v1 on v0

v1 whole, which is shorter than its diff:
```python
import functools

import jax
import jax.numpy as jnp
from jax import lax
from jax.experimental import pallas as pl
from jax.experimental.pallas import tpu as pltpu
from jax.sharding import PartitionSpec as P

EXPERTS = 4
TOP = 2
LANES = 128
F32 = jnp.float32
BF16 = jnp.bfloat16
VMEM = pl.BlockSpec(memory_space=pltpu.VMEM)
ANY = pl.BlockSpec(memory_space=pl.ANY)
SMEM = pl.BlockSpec(memory_space=pltpu.SMEM)
MIB = 1 << 20


def tile(size, want):
    while size % want:
        want //= 2
    return want


def rounds(width, hidden):
    return min(width // tile(width, 1024), hidden // tile(hidden, LANES))


def nt(left, right):
    return lax.dot_general(left, right, (((1,), (1,)), ((), ())), preferred_element_type=F32)


def tn(left, right):
    return lax.dot_general(left, right, (((0,), (0,)), ((), ())), preferred_element_type=F32)


def split_sum(value):
    high = value.astype(BF16)
    return high, (value - high.astype(F32)).astype(BF16)


def write_outer(left_ref, right_ref, out_ref, slots, sems, rows, step, steps):
    count = slots.shape[0]
    slot = lax.rem(step, count)
    start = pl.multiple_of(step * rows, rows)

    def copy(index, at):
        return pltpu.make_async_copy(slots.at[index], out_ref.at[0, pl.ds(at, rows)], sems.at[index])

    @pl.when(step >= count)
    def _():
        copy(slot, pl.multiple_of((step - count) * rows, rows)).wait()

    slots[slot] = tn(left_ref[:, pl.ds(start, rows)], right_ref).astype(BF16)
    copy(slot, start).start()


def drain(out_ref, slots, sems, rows, steps):
    count = slots.shape[0]
    for step in range(max(0, steps - count), steps):
        index = step % count
        pltpu.make_async_copy(slots.at[index], out_ref.at[0, pl.ds(step * rows, rows)], sems.at[index]).wait()


def main_kernel(
    width, block, expert_ref, rows_ref, wg_ref, wu_ref, wd_ref,
    keep_ref, send_ref, dg_ref, du_ref, gd_ref, weighted, score, slots, sems,
):
    count = rows_ref.shape[0]
    hidden = wg_ref.shape[2]
    extra = rows_ref[:, 2 * width :].astype(F32)
    lane = lax.broadcasted_iota(jnp.int32, extra.shape, 1)
    mine = jnp.where(lane // TOP == expert_ref[0], extra, 0.0)
    scale = jnp.sum(mine, axis=1, keepdims=True)
    score[...] = jnp.zeros_like(score)
    part = tile(hidden, 1024)

    @pl.loop(0, hidden // part)
    def _(step):
        at = pl.ds(pl.multiple_of(step * part, part), part)
        gate = jnp.dot(rows_ref[:, :width], wg_ref[0, :, at], preferred_element_type=F32)
        up = jnp.dot(rows_ref[:, :width], wu_ref[0, :, at], preferred_element_type=F32)
        back = nt(rows_ref[:, width : 2 * width], wd_ref[0, at, :])
        sigma = jax.nn.sigmoid(gate)
        act = gate * sigma
        slope = sigma * (1.0 + gate * (1.0 - sigma))
        hid = act * up
        score[...] += jnp.sum(back * hid, axis=1, keepdims=True)
        scaled = scale * back
        dg_ref[:, at] = (scaled * up * slope).astype(BF16)
        du_ref[:, at] = (scaled * act).astype(BF16)
        weighted[:, at] = (scale * hid).astype(BF16)

    slot_score = jnp.where(mine > 0.0, score[...], 0.0)
    keep_ref[:, width:] = slot_score[:block]
    high, low = split_sum(slot_score[block:])
    send_ref[:, width : width + LANES] = high
    send_ref[:, width + LANES :] = low

    steps = rounds(width, hidden)
    across = width // steps
    pieces = hidden // steps // slots.shape[1]

    @pl.loop(0, steps)
    def _(step):
        at = pl.ds(pl.multiple_of(step * across, across), across)
        total = nt(dg_ref[...], wg_ref[0, at, :]) + nt(du_ref[...], wu_ref[0, at, :])
        keep_ref[:, at] = total[:block]
        send_ref[:, at] = total[block:].astype(BF16)
        for piece in range(pieces):
            write_outer(
                weighted, rows_ref[:, width : 2 * width], gd_ref, slots, sems, slots.shape[1],
                step * pieces + piece, steps * pieces,
            )

    drain(gd_ref, slots, sems, slots.shape[1], steps * pieces)


def main_call(expert, rows, w_gate, w_up, w_down, block):
    count = rows.shape[0]
    _, width, hidden = w_gate.shape
    w_gate, w_up, w_down = (pltpu.with_memory_space_constraint(w, pltpu.VMEM) for w in (w_gate, w_up, w_down))
    down = tile(hidden // rounds(width, hidden), 256)
    room = 60 * MIB - 3 * 2 * width * hidden
    flops = 2 * count * width * hidden * 6
    return pl.pallas_call(
        functools.partial(main_kernel, width, block),
        out_shape=(
            jax.ShapeDtypeStruct((block, width + LANES), F32),
            jax.ShapeDtypeStruct((count - block, width + 2 * LANES), BF16),
            jax.ShapeDtypeStruct((count, hidden), BF16),
            jax.ShapeDtypeStruct((count, hidden), BF16),
            jax.ShapeDtypeStruct(w_down.shape, BF16),
        ),
        in_specs=[SMEM, VMEM, VMEM, VMEM, VMEM],
        out_specs=(VMEM, VMEM, VMEM, VMEM, ANY),
        scratch_shapes=[
            pltpu.VMEM((count, hidden), BF16),
            pltpu.VMEM((count, 1), F32),
            pltpu.VMEM((2, down, width), BF16),
            pltpu.SemaphoreType.DMA((2,)),
        ],
        compiler_params=pltpu.CompilerParams(vmem_limit_bytes=room),
        cost_estimate=pl.CostEstimate(flops=flops, bytes_accessed=2 * 4 * width * hidden, transcendentals=count * hidden),
        name="hidden_and_inputs",
    )(expert, rows, w_gate, w_up, w_down)


def outer_kernel(width, rows_ref, right_ref, out_ref, slots, sems):
    size = slots.shape[1]
    steps = width // size

    @pl.loop(0, steps)
    def _(step):
        write_outer(rows_ref, right_ref[...], out_ref, slots, sems, size, step, steps)

    drain(out_ref, slots, sems, size, steps)


def outer_call(rows, right, width, name):
    count, hidden = right.shape
    size = tile(width, 512)
    return pl.pallas_call(
        functools.partial(outer_kernel, width),
        out_shape=jax.ShapeDtypeStruct((1, width, hidden), BF16),
        in_specs=[VMEM, VMEM],
        out_specs=ANY,
        scratch_shapes=[pltpu.VMEM((3, size, hidden), BF16), pltpu.SemaphoreType.DMA((3,))],
        compiler_params=pltpu.CompilerParams(vmem_limit_bytes=24 * MIB),
        cost_estimate=pl.CostEstimate(
            flops=2 * count * width * hidden * 4, bytes_accessed=2 * width * hidden, transcendentals=0
        ),
        name=name,
    )(rows, right)


def fold_kernel(width, block, have_ref, *refs):
    received, (keep_ref, send_ref) = refs[:-2], refs[-2:]
    total = have_ref[:, :width]
    slot = have_ref[:, width:]
    for ref in received:
        total += ref[:, :width].astype(F32)
        slot += ref[:, width : width + LANES].astype(F32) + ref[:, width + LANES :].astype(F32)
    keep_ref[:, :width] = total[:block]
    keep_ref[:, width:] = slot[:block]
    send_ref[:, :width] = total[block:].astype(BF16)
    high, low = split_sum(slot[block:])
    send_ref[:, width : width + LANES] = high
    send_ref[:, width + LANES :] = low


def fold(have, received, block, width):
    return pl.pallas_call(
        functools.partial(fold_kernel, width, block),
        out_shape=(
            jax.ShapeDtypeStruct((block, width + LANES), F32),
            jax.ShapeDtypeStruct((have.shape[0] - block, width + 2 * LANES), BF16),
        ),
        in_specs=[VMEM] * (1 + len(received)),
        out_specs=(VMEM, VMEM),
        name="fold",
    )(have, *received)


def last_kernel(width, have_ref, *refs):
    received, (dx_ref, slot_ref) = refs[:-2], refs[-2:]
    total = have_ref[:, :width]
    slot = have_ref[:, width:]
    for ref in received:
        total += ref[:, :width].astype(F32)
        slot += ref[:, width : width + LANES].astype(F32) + ref[:, width + LANES :].astype(F32)
    dx_ref[...] = total
    slot_ref[...] = slot


def last(have, received, width):
    return pl.pallas_call(
        functools.partial(last_kernel, width),
        out_shape=(
            jax.ShapeDtypeStruct((have.shape[0], width), F32),
            jax.ShapeDtypeStruct((have.shape[0], LANES), F32),
        ),
        in_specs=[VMEM] * (1 + len(received)),
        out_specs=(VMEM, VMEM),
        name="last",
    )(have, *received)


def shift(value, axis, by):
    size = lax.axis_size(axis)
    return lax.ppermute(value, axis, [(i, (i + by) % size) for i in range(size)])


def spread(block, axis):
    size = lax.axis_size(axis)
    return jnp.concatenate([block] + [shift(block, axis, by) for by in range(1, size)], axis=0)


def collect(send, axis, block):
    size = lax.axis_size(axis)
    return [shift(send[(by - 1) * block : by * block], axis, -by) for by in range(1, size)]


def per_device(tokens, out_grad, expert_ids, probs, w_gate, w_up, w_down):
    count, width = tokens.shape
    owners = lax.axis_size("expert")
    expert = (lax.axis_index("expert") // (owners // EXPERTS)).astype(jnp.int32).reshape(1)
    lane = jnp.arange(LANES, dtype=jnp.int32)[None, :]
    extra = jnp.zeros((count, LANES), BF16)
    for k in range(TOP):
        hit = lane == expert_ids[:, k : k + 1] * TOP + k
        extra = jnp.where(hit, probs[:, k : k + 1], extra)
    rows = jnp.concatenate([tokens, out_grad, extra], axis=1)
    for axis in ("expert", "tensor", "seq"):
        rows = spread(rows, axis)
    block = rows.shape[0] // lax.axis_size("seq")
    keep, send, d_gate, d_up, grad_d = main_call(expert, rows, w_gate, w_up, w_down, block)
    received = collect(send, "seq", block)
    block //= lax.axis_size("tensor")
    keep, send = fold(keep, received, block, width)
    received = collect(send, "tensor", block)
    grad_g = outer_call(rows, d_gate, width, "outer_gate")
    block //= owners
    keep, send = fold(keep, received, block, width)
    received = collect(send, "expert", block)
    grad_u = outer_call(rows, d_up, width, "outer_up")
    grad_tokens, slot = last(keep, received, width)
    grad_probs = jnp.sum(slot[:, : EXPERTS * TOP].reshape(count, EXPERTS, TOP), axis=1)
    return (grad_tokens, grad_probs, grad_g, grad_u, grad_d)


def solution(mesh):
    placed = (
        P(("parts", "expert", "tensor", "seq"), None),
        P(("parts", "expert", "tensor", "seq"), None),
        P(("parts", "expert", "tensor", "seq"), None),
        P(("parts", "expert", "tensor", "seq"), None),
        P("expert", None, ("tensor", "seq")),
        P("expert", None, ("tensor", "seq")),
        P("expert", ("tensor", "seq"), None),
    )
    return jax.shard_map(
        per_device,
        mesh=mesh,
        in_specs=placed,
        out_specs=(
            P(("parts", "expert", "tensor", "seq"), None),
            P(("parts", "expert", "tensor", "seq"), None),
            P(("parts", "expert"), None, ("tensor", "seq")),
            P(("parts", "expert"), None, ("tensor", "seq")),
            P(("parts", "expert"), ("tensor", "seq"), None),
        ),
        check_vma=False,
    )
```

time: 132 us -> 116 us (0.88)
  matrix products: 71.8 us -> 0 us
  Pallas kernels: 0 us -> 51.6 us
  local copies, waits for them, and re-layouts: 11.8 us -> 30.3 us
  starting transfers between devices: 26.8 us -> 13.8 us
  waiting for transfers between devices: 19 us -> 15.8 us
  other arithmetic: 1.51 us -> 3.15 us
    dot_general x10 -> x0, matrix products: 71.8 us -> none  [the longest x6 58.5 us: contract(): lax.dot_general(left, right, (((left_dim,), (right_dim,)), ((), ())), pre...]
    pallas_call x0 -> x6, Pallas kernels: none -> 51.6 us  [the longest x1 31.9 us: main_call(): pl.pallas_call(functools.partial(main_kernel, width, block), out_shape=(j...]
    all_to_all x5 -> x0, starting transfers between devices: 26.8 us -> none  [the longest x1 7.39 us: per_device(): lax.all_to_all(repeat_owners(packed_p, fanout), ('expert', 'tensor', 'seq...]
    all_to_all x5 -> x0, waiting for transfers between devices: 19 us -> none  [the longest x1 12.9 us: per_device(): lax.all_to_all(repeat_owners(packed_x, fanout), ('expert', 'tensor', 'seq...]
    unnamed x12 -> x22, local copies, waits for them, and re-layouts: 3.05 us -> 20.2 us
    ppermute x0 -> x10, waiting for transfers between devices: none -> 15.8 us  [shift(): lax.ppermute(value, axis, [(i, (i + by) % size) for i in range(size)])]
    ppermute x0 -> x10, starting transfers between devices: none -> 13.8 us  [shift(): lax.ppermute(value, axis, [(i, (i + by) % size) for i in range(size)])]
    concatenate x0 -> x2, local copies, waits for them, and re-layouts: none -> 7.63 us  [spread(): jnp.concatenate([block] + [shift(block, axis, by) for by in range(1, size...]
  transfers between devices with their start and end apart: 5 -> 10, of which waited for: 3 -> 5; matrix products, arithmetic and copies ran while one was open for 49% -> 0% of each run, Pallas kernels for 0% -> 13%
where the time goes in v1:
time: 116 us; the launch traced here: 115 us
  Pallas kernels  51.6 us (44%)
  local copies, waits for them, and re-layouts  30.3 us (26%)
  waiting for transfers between devices  15.8 us (14%)
  starting transfers between devices  13.8 us (12%)
  other arithmetic  3.15 us (3%)
    pallas_call x1, Pallas kernels, main_call(): pl.pallas_call(functools.partial(main_kernel, width, block), out_shape=(j...  31.9 us
    unnamed x22, local copies, waits for them, and re-layouts  20.2 us
    ppermute x10, waiting for transfers between devices, shift(): lax.ppermute(value, axis, [(i, (i + by) % size) for i in range(size)])  15.8 us
    pallas_call x2, Pallas kernels, outer_call(): pl.pallas_call(functools.partial(outer_kernel, width), out_shape=jax.Shap...  14.5 us
    ppermute x10, starting transfers between devices, shift(): lax.ppermute(value, axis, [(i, (i + by) % size) for i in range(size)])  13.8 us
    concatenate x2, local copies, waits for them, and re-layouts, spread(): jnp.concatenate([block] + [shift(block, axis, by) for by in range(1, size...  7.63 us
    pallas_call x2, Pallas kernels, fold(): pl.pallas_call(functools.partial(fold_kernel, width, block), out_shape=(j...  3.6 us
  transfers between devices with their start and end apart: 10, of which 5 were waited for; matrix products, arithmetic and copies ran while one was open for 0% of the time, Pallas kernels for 13%

profile of v1, /device:TPU:0, one launch (start us, length us, event | category | flops | bytes accessed | tf_op | source)
XLA Modules:
  0.0 115.4 jit_solution(5153546783536045001)
XLA Ops:
  0.6 0.8 add_bitcast_fusion
  1.4 0.7 slice_bitcast_fusion.1
  2.1 0.1 fusion
  2.2 0.8 pad_maximum_fusion.1
  3.0 5.1 %collective-permute-start.2 = (bf16[4,8320]{1,0:T(4,128)(2,1)S(1)}, bf16[4,8320]{1,0:T(4,128)(2,1)S(1)}, u32[]{:S(2)}, u32[]{:S(2)}) collective-permute-start(bf16[4,8320]{1,0:T(4,128)(2,1)S(1)} %pad_maximum_fusion.1), channel_id=1, source_target_pairs={{0,12},{4,0},{8,4},{12,8},{1,13},{5,1},{9,5},{13,9},{2,14},{6,2},{... | collective-permute-start | bytes 199688 | tf_op jit(solution)/shard_map/ppermute | solution.py:233
  8.1 0.0 collective-permute-start.1
  8.1 1.0 collective-permute-start
  9.2 1.5 %collective-permute-done.2 = bf16[4,8320]{1,0:T(4,128)(2,1)S(1)} collective-permute-done((bf16[4,8320]{1,0:T(4,128)(2,1)S(1)}, bf16[4,8320]{1,0:T(4,128)(2,1)S(1)}, u32[]{:S(2)}, u32[]{:S(2)}) %collective-permute-start.2) | collective-permute-done | bytes 66592 | tf_op jit(solution)/shard_map/ppermute | solution.py:233
  10.6 4.1 %collective-permute-done.1 = bf16[4,8320]{1,0:T(4,128)(2,1)S(1)} collective-permute-done((bf16[4,8320]{1,0:T(4,128)(2,1)S(1)}, bf16[4,8320]{1,0:T(4,128)(2,1)S(1)}, u32[]{:S(2)}, u32[]{:S(2)}) %collective-permute-start.1) | collective-permute-done | bytes 66592 | tf_op jit(solution)/shard_map/ppermute | solution.py:233
  14.7 0.0 collective-permute-done
  14.7 0.9 pad_maximum_fusion
  15.6 1.6 %collective-permute-start.3 = (bf16[16,8320]{1,0:T(8,128)(2,1)S(1)}, bf16[16,8320]{1,0:T(8,128)(2,1)S(1)}, u32[]{:S(2)}, u32[]{:S(2)}) collective-permute-start(bf16[16,8320]{1,0:T(8,128)(2,1)S(1)} %pad_maximum_fusion), channel_id=1, source_target_pairs={{0,2},{2,0},{1,3},{3,1},{4,6},{6,4},{5,7},{7,5},{8,10},{10,8},{9,1... | collective-permute-start | bytes 798728 | tf_op jit(solution)/shard_map/ppermute | solution.py:233
  17.2 6.7 %collective-permute-done.3 = bf16[16,8320]{1,0:T(8,128)(2,1)S(1)} collective-permute-done((bf16[16,8320]{1,0:T(8,128)(2,1)S(1)}, bf16[16,8320]{1,0:T(8,128)(2,1)S(1)}, u32[]{:S(2)}, u32[]{:S(2)}) %collective-permute-start.3) | collective-permute-done | bytes 266272 | tf_op jit(solution)/shard_map/ppermute | solution.py:233
  23.9 2.1 %concatenate.16 = bf16[32,8320]{1,0:T(8,128)(2,1)S(1)} concatenate(bf16[4,8320]{1,0:T(4,128)(2,1)S(1)} %pad_maximum_fusion.1, bf16[4,8320]{1,0:T(4,128)(2,1)S(1)} %collective-permute-done, bf16[4,8320]{1,0:T(4,128)(2,1)S(1)} %collective-permute-done.1, bf16[4,8320]{1,0:T(4,128)(2,1)S(1)} %collective-permute-done.2, bf16[16,8320]{1,0:T(8,128)(2,1)S(1)} %collective-permute-done.3), dimensions={0} | concatenate | bytes 1064960 | tf_op jit(solution)/shard_map/concatenate | solution.py:238
  26.0 0.1 collective-permute-start.4
  26.1 1.9 %collective-permute-done.4 = bf16[32,8320]{1,0:T(8,128)(2,1)S(1)} collective-permute-done((bf16[32,8320]{1,0:T(8,128)(2,1)S(1)}, bf16[32,8320]{1,0:T(8,128)(2,1)S(1)}, u32[]{:S(2)}, u32[]{:S(2)}) %collective-permute-start.4) | collective-permute-done | bytes 532512 | tf_op jit(solution)/shard_map/ppermute | solution.py:233
  28.0 5.5 %concatenate.17.rows_ref = bf16[64,8320]{1,0:T(8,128)(2,1)} concatenate(bf16[4,8320]{1,0:T(4,128)(2,1)S(1)} %pad_maximum_fusion.1, bf16[4,8320]{1,0:T(4,128)(2,1)S(1)} %collective-permute-done, bf16[4,8320]{1,0:T(4,128)(2,1)S(1)} %collective-permute-done.1, bf16[4,8320]{1,0:T(4,128)(2,1)S(1)} %collective-permute-done.2, bf16[16,8320]{1,0:T(8,128)(2,1)S(1)} %collective-permute-done.3, ...), dimensions={0} | concatenate | bytes 2129920 | tf_op jit(solution)/shard_map/concatenate | solution.py:238
  33.5 5.8 %copy-done.1 = bf16[1,4096,2048]{2,1,0:T(8,128)(2,1)S(1)} copy-done((bf16[1,4096,2048]{2,1,0:T(8,128)(2,1)S(1)}, bf16[1,4096,2048]{2,1,0:T(8,128)(2,1)}, u32[]{:S(2)}) %copy-start.1) | copy-done | bytes 16777240
  39.3 5.8 %copy-done.2 = bf16[1,4096,2048]{2,1,0:T(8,128)(2,1)S(1)} copy-done((bf16[1,4096,2048]{2,1,0:T(8,128)(2,1)S(1)}, bf16[1,4096,2048]{2,1,0:T(8,128)(2,1)}, u32[]{:S(2)}) %copy-start.2) | copy-done | bytes 16777240
  45.0 5.8 %copy-done.3 = bf16[1,2048,4096]{2,1,0:T(8,128)(2,1)S(1)} copy-done((bf16[1,2048,4096]{2,1,0:T(8,128)(2,1)S(1)}, bf16[1,2048,4096]{2,1,0:T(8,128)(2,1)}, u32[]{:S(2)}) %copy-start.3) | copy-done | bytes 16777240
  50.8 31.9 %hidden_and_inputs.1 = (f32[32,4224]{1,0:T(8,128)}, bf16[32,4352]{1,0:T(8,128)(2,1)}, bf16[64,2048]{1,0:T(8,128)(2,1)}, bf16[64,2048]{1,0:T(8,128)(2,1)}, bf16[1,2048,4096]{2,1,0:T(8,128)(2,1)}) custom-call(s32[1]{0:T(128)} %bitcast.expert_ref, bf16[64,8320]{1,0:T(8,128)(2,1)} %concatenate.17.rows_ref, bf16[1,4096,2048]{2,1,0:T(8,128)(2,1)S(1)} %copy-done.1, ...), custom_call_target="tpu_custom_call" | custom-call | flops 6442450944 | bytes 67108864 | tf_op jit(solution)/shard_map/hidden_and_inputs/pallas_call | solution.py:128
  82.7 0.2 collective-permute-start.5
  82.9 1.6 %collective-permute-done.5.refs_0_ = bf16[32,4352]{1,0:T(8,128)(2,1)S(1)} collective-permute-done((bf16[32,4352]{1,0:T(8,128)(2,1)}, bf16[32,4352]{1,0:T(8,128)(2,1)S(1)}, u32[]{:S(2)}, u32[]{:S(2)}) %collective-permute-start.5) | collective-permute-done | bytes 278560 | tf_op jit(solution)/shard_map/ppermute | solution.py:233
  84.5 0.7 copy-done.6
  85.2 1.9 %fold.2 = (f32[16,4224]{1,0:T(8,128)}, bf16[16,4352]{1,0:T(8,128)(2,1)}) custom-call(f32[32,4224]{1,0:T(8,128)} %get-tuple-element.16.have_ref, bf16[32,4352]{1,0:T(8,128)(2,1)} %copy-done.6), custom_call_target="tpu_custom_call" | custom-call | tf_op jit(solution)/shard_map/fold/pallas_call | solution.py:195
  87.1 1.5 %collective-permute-start.6 = (bf16[16,4352]{1,0:T(8,128)(2,1)}, bf16[16,4352]{1,0:T(8,128)(2,1)S(1)}, u32[]{:S(2)}, u32[]{:S(2)}) collective-permute-start(bf16[16,4352]{1,0:T(8,128)(2,1)} %get-tuple-element.19), channel_id=1, source_target_pairs={{0,2},{2,0},{1,3},{3,1},{4,6},{6,4},{5,7},{7,5},{8,10},{10,8},{9,1... | collective-permute-start | bytes 417800 | tf_op jit(solution)/shard_map/ppermute | solution.py:233
  88.6 0.9 copy-done.5
  89.6 7.3 %outer_gate.1 = bf16[1,4096,2048]{2,1,0:T(8,128)(2,1)} custom-call(bf16[64,8320]{1,0:T(8,128)(2,1)S(1)} %copy-done, bf16[64,2048]{1,0:T(8,128)(2,1)S(1)} %copy-done.5), custom_call_target="tpu_custom_call" | custom-call | flops 4294967296 | bytes 16777216 | tf_op jit(solution)/shard_map/outer_gate/pallas_call | solution.py:165
  96.9 0.0 collective-permute-done.6.refs_0_
  96.9 0.0 copy-start.7
  96.9 0.6 copy-done.7
  97.5 1.7 %fold.3 = (f32[4,4224]{1,0:T(4,128)}, bf16[12,4352]{1,0:T(8,128)(2,1)}) custom-call(f32[16,4224]{1,0:T(8,128)} %get-tuple-element.18.have_ref, bf16[16,4352]{1,0:T(8,128)(2,1)} %copy-done.7), custom_call_target="tpu_custom_call" | custom-call | tf_op jit(solution)/shard_map/fold/pallas_call | solution.py:195
  99.2 1.0 fusion.2
  100.2 0.1 collective-permute-start.9
  100.3 1.4 %collective-permute-start.8 = (bf16[4,4352]{1,0:T(4,128)(2,1)S(1)}, bf16[4,4352]{1,0:T(4,128)(2,1)S(1)}, u32[]{:S(2)}, u32[]{:S(2)}) collective-permute-start(bf16[4,4352]{1,0:T(4,128)(2,1)S(1)} %get-tuple-element.28), channel_id=1, source_target_pairs={{0,8},{4,12},{8,0},{12,4},{1,9},{5,13},{9,1},{13,5},{2,10},{6,14},... | collective-permute-start | bytes 104456 | tf_op jit(solution)/shard_map/ppermute | solution.py:233
  101.7 2.8 %collective-permute-start.7 = (bf16[4,4352]{1,0:T(4,128)(2,1)S(1)}, bf16[4,4352]{1,0:T(4,128)(2,1)S(1)}, u32[]{:S(2)}, u32[]{:S(2)}) collective-permute-start(bf16[4,4352]{1,0:T(4,128)(2,1)S(1)} %get-tuple-element.29), channel_id=1, source_target_pairs={{0,12},{4,0},{8,4},{12,8},{1,13},{5,1},{9,5},{13,9},{2,14},{6,2},{... | collective-permute-start | bytes 104456 | tf_op jit(solution)/shard_map/ppermute | solution.py:233
  104.6 0.0 copy-done.4
  104.6 7.3 %outer_up.1 = bf16[1,4096,2048]{2,1,0:T(8,128)(2,1)} custom-call(bf16[64,8320]{1,0:T(8,128)(2,1)S(1)} %copy-done, bf16[64,2048]{1,0:T(8,128)(2,1)S(1)} %copy-done.4), custom_call_target="tpu_custom_call" | custom-call | flops 4294967296 | bytes 16777216 | tf_op jit(solution)/shard_map/outer_up/pallas_call | solution.py:165
  111.9 0.0 collective-permute-done.9.refs_2_
  111.9 0.0 collective-permute-done.8.refs_1_
  111.9 0.0 collective-permute-done.7.refs_0_
  111.9 0.0 copy-start.10
  111.9 0.6 copy-done.8
  112.5 0.0 copy-done.9
  112.5 0.0 copy-done.10
  112.5 1.6 %last.1 = (f32[4,4096]{1,0:T(4,128)}, f32[4,128]{1,0:T(4,128)}) custom-call(f32[4,4224]{1,0:T(4,128)} %get-tuple-element.20.have_ref, bf16[4,4352]{1,0:T(4,128)(2,1)} %copy-done.10, bf16[4,4352]{1,0:T(4,128)(2,1)} %copy-done.9, bf16[4,4352]{1,0:T(4,128)(2,1)} %copy-done.8), custom_call_target="tpu_custom_call" | custom-call | tf_op jit(solution)/shard_map/last/pallas_call | solution.py:219
  114.1 0.7 copy.12
  114.8 0.6 reduce_sum.9
  (10 shorter events, 0.0 us)
Async XLA Ops:
  3.0 7.6 %collective-permute-start.2 = (bf16[4,8320]{1,0:T(4,128)(2,1)S(1)}, bf16[4,8320]{1,0:T(4,128)(2,1)S(1)}, u32[]{:S(2)}, u32[]{:S(2)}) collective-permute-start(bf16[4,8320]{1,0:T(4,128)(2,1)S(1)} %pad_maximum_fusion.1), channel_id=1, source_target_pairs={{0,12},{4,0},{8,4},{12,8},{1,13},{5,1},{9,5},{13,9},{2,14},{6,2},{... | collective-permute-start | bytes 199688 | tf_op jit(solution)/shard_map/ppermute | solution.py:233
  8.1 6.6 %collective-permute-start.1 = (bf16[4,8320]{1,0:T(4,128)(2,1)S(1)}, bf16[4,8320]{1,0:T(4,128)(2,1)S(1)}, u32[]{:S(2)}, u32[]{:S(2)}) collective-permute-start(bf16[4,8320]{1,0:T(4,128)(2,1)S(1)} %pad_maximum_fusion.1), channel_id=1, source_target_pairs={{0,8},{4,12},{8,0},{12,4},{1,9},{5,13},{9,1},{13,5},{2,10},{6,14},... | collective-permute-start | bytes 199688 | tf_op jit(solution)/shard_map/ppermute | solution.py:233
  8.1 6.6 %collective-permute-start = (bf16[4,8320]{1,0:T(4,128)(2,1)S(1)}, bf16[4,8320]{1,0:T(4,128)(2,1)S(1)}, u32[]{:S(2)}, u32[]{:S(2)}) collective-permute-start(bf16[4,8320]{1,0:T(4,128)(2,1)S(1)} %pad_maximum_fusion.1), channel_id=1, source_target_pairs={{0,4},{4,8},{8,12},{12,0},{1,5},{5,9},{9,13},{13,1},{2,6},{6,10},{... | collective-permute-start | bytes 199688 | tf_op jit(solution)/shard_map/ppermute | solution.py:233
  15.6 8.2 %collective-permute-start.3 = (bf16[16,8320]{1,0:T(8,128)(2,1)S(1)}, bf16[16,8320]{1,0:T(8,128)(2,1)S(1)}, u32[]{:S(2)}, u32[]{:S(2)}) collective-permute-start(bf16[16,8320]{1,0:T(8,128)(2,1)S(1)} %pad_maximum_fusion), channel_id=1, source_target_pairs={{0,2},{2,0},{1,3},{3,1},{4,6},{6,4},{5,7},{7,5},{8,10},{10,8},{9,1... | collective-permute-start | bytes 798728 | tf_op jit(solution)/shard_map/ppermute | solution.py:233
  26.0 2.0 %collective-permute-start.4 = (bf16[32,8320]{1,0:T(8,128)(2,1)S(1)}, bf16[32,8320]{1,0:T(8,128)(2,1)S(1)}, u32[]{:S(2)}, u32[]{:S(2)}) collective-permute-start(bf16[32,8320]{1,0:T(8,128)(2,1)S(1)} %concatenate.16), channel_id=1, source_target_pairs={{0,1},{1,0},{2,3},{3,2},{4,5},{5,4},{6,7},{7,6},{8,9},{9,8},{10,11... | collective-permute-start | bytes 1597448 | tf_op jit(solution)/shard_map/ppermute | solution.py:233
  33.5 5.8 %copy-start.1 = (bf16[1,4096,2048]{2,1,0:T(8,128)(2,1)S(1)}, bf16[1,4096,2048]{2,1,0:T(8,128)(2,1)}, u32[]{:S(2)}) copy-start(bf16[1,4096,2048]{2,1,0:T(8,128)(2,1)} %wg_ref.1) | copy-start | bytes 50331652
  39.3 5.8 %copy-start.2 = (bf16[1,4096,2048]{2,1,0:T(8,128)(2,1)S(1)}, bf16[1,4096,2048]{2,1,0:T(8,128)(2,1)}, u32[]{:S(2)}) copy-start(bf16[1,4096,2048]{2,1,0:T(8,128)(2,1)} %wu_ref.1) | copy-start | bytes 50331652
  45.0 5.8 %copy-start.3 = (bf16[1,2048,4096]{2,1,0:T(8,128)(2,1)S(1)}, bf16[1,2048,4096]{2,1,0:T(8,128)(2,1)}, u32[]{:S(2)}) copy-start(bf16[1,2048,4096]{2,1,0:T(8,128)(2,1)} %wd_ref.1) | copy-start | bytes 50331652
  50.8 37.8 %copy-start = (bf16[64,8320]{1,0:T(8,128)(2,1)S(1)}, bf16[64,8320]{1,0:T(8,128)(2,1)}, u32[]{:S(2)}) copy-start(bf16[64,8320]{1,0:T(8,128)(2,1)} %concatenate.17.rows_ref) | copy-start | bytes 3194884
  82.7 21.9 %copy-start.4 = (bf16[64,2048]{1,0:T(8,128)(2,1)S(1)}, bf16[64,2048]{1,0:T(8,128)(2,1)}, u32[]{:S(2)}) copy-start(bf16[64,2048]{1,0:T(8,128)(2,1)} %get-tuple-element.25.right_ref) | copy-start | bytes 786436
  82.7 1.8 %collective-permute-start.5 = (bf16[32,4352]{1,0:T(8,128)(2,1)}, bf16[32,4352]{1,0:T(8,128)(2,1)S(1)}, u32[]{:S(2)}, u32[]{:S(2)}) collective-permute-start(bf16[32,4352]{1,0:T(8,128)(2,1)} %get-tuple-element.17), channel_id=1, source_target_pairs={{0,1},{1,0},{2,3},{3,2},{4,5},{5,4},{6,7},{7,6},{8,9},{9,8},{10,11... | collective-permute-start | bytes 835592 | tf_op jit(solution)/shard_map/ppermute | solution.py:233
  84.5 0.7 copy-start.6
  87.1 9.7 %collective-permute-start.6 = (bf16[16,4352]{1,0:T(8,128)(2,1)}, bf16[16,4352]{1,0:T(8,128)(2,1)S(1)}, u32[]{:S(2)}, u32[]{:S(2)}) collective-permute-start(bf16[16,4352]{1,0:T(8,128)(2,1)} %get-tuple-element.19), channel_id=1, source_target_pairs={{0,2},{2,0},{1,3},{3,1},{4,6},{6,4},{5,7},{7,5},{8,10},{10,8},{9,1... | collective-permute-start | bytes 417800 | tf_op jit(solution)/shard_map/ppermute | solution.py:233
  88.6 1.0 copy-start.5
  96.9 0.7 copy-start.7
  100.2 11.6 %collective-permute-start.9 = (bf16[4,4352]{1,0:T(4,128)(2,1)S(1)}, bf16[4,4352]{1,0:T(4,128)(2,1)S(1)}, u32[]{:S(2)}, u32[]{:S(2)}) collective-permute-start(bf16[4,4352]{1,0:T(4,128)(2,1)S(1)} %get-tuple-element.27), channel_id=1, source_target_pairs={{0,4},{4,8},{8,12},{12,0},{1,5},{5,9},{9,13},{13,1},{2,6},{6,10},{... | collective-permute-start | bytes 104456 | tf_op jit(solution)/shard_map/ppermute | solution.py:233
  100.3 11.6 %collective-permute-start.8 = (bf16[4,4352]{1,0:T(4,128)(2,1)S(1)}, bf16[4,4352]{1,0:T(4,128)(2,1)S(1)}, u32[]{:S(2)}, u32[]{:S(2)}) collective-permute-start(bf16[4,4352]{1,0:T(4,128)(2,1)S(1)} %get-tuple-element.28), channel_id=1, source_target_pairs={{0,8},{4,12},{8,0},{12,4},{1,9},{5,13},{9,1},{13,5},{2,10},{6,14},... | collective-permute-start | bytes 104456 | tf_op jit(solution)/shard_map/ppermute | solution.py:233
  101.7 10.2 %collective-permute-start.7 = (bf16[4,4352]{1,0:T(4,128)(2,1)S(1)}, bf16[4,4352]{1,0:T(4,128)(2,1)S(1)}, u32[]{:S(2)}, u32[]{:S(2)}) collective-permute-start(bf16[4,4352]{1,0:T(4,128)(2,1)S(1)} %get-tuple-element.29), channel_id=1, source_target_pairs={{0,12},{4,0},{8,4},{12,8},{1,13},{5,1},{9,5},{13,9},{2,14},{6,2},{... | collective-permute-start | bytes 104456 | tf_op jit(solution)/shard_map/ppermute | solution.py:233
  111.9 0.6 copy-start.8
  111.9 0.6 copy-start.9
  111.9 0.6 copy-start.10
